TPU v7x, 32 devices: a whole 2x2x4 slice. The times are simulated.
32 devices in a mesh: rcv: 4 (over z), src: 8 (over y, x, core).
Axes of the slice: x: 2, y: 2, z: 4, core: 2. Of those that a mesh axis runs over, the one named last changes fastest.
Arguments:
- reflection: bfloat16 [2, 16384, 16384], P(None, 'rcv', 'src'), may hold values from -6 to 6
- green: bfloat16 [2, 16384, 512], P(None, 'rcv', 'src'), may hold values from -0.046875 to 0.046875
- tile_mask: int32 [64, 64], replicated, may hold values from 0 to 1, as said below
- reference_index: int32 [512], P(('rcv', 'src')), may hold values from 0 to 511
Outputs:
- aligned: float32 [512, 2, 512], P(('rcv', 'src'))
Inputs may be any that keep to these rules, and one draw needn't show every extreme that they name: `tile_mask`: entries below the diagonal are 0.
All inputs are finite; a program needn't handle non-finite values.
Results may differ from a plain program's by a relative error of at most 0.02.
Values may be sent and summed in bfloat16 or wider, within the bound.
A program may use at most 256 MiB of HBM per device.

v0:
```python
import jax
import jax.numpy as jnp
from jax import lax
from jax.sharding import PartitionSpec as P

P_SIZE = 512
TILE = 256


def broadcast(block, axis, holder):
    block = jnp.where(lax.axis_index(axis) == holder, block, jnp.zeros_like(block))
    return lax.psum(block, axis)


def across(first, second, precision=None):
    return lax.dot_general(
        first,
        second,
        (((0,), (0,)), ((), ())),
        precision=precision,
        preferred_element_type=jnp.float32,
    )


def body(reflection, green, tile_mask, reference_index):
    rows_blk = reflection.shape[1]
    col_count = reflection.shape[2]
    rcv_index = lax.axis_index("rcv")
    src_index = lax.axis_index("src")
    green_block = lax.all_gather(green, "src", axis=2, tiled=True)
    src_per_rcv = lax.axis_size("src") // lax.axis_size("rcv")
    green_piece = lax.dynamic_slice_in_dim(
        green_block, src_index % src_per_rcv * col_count, col_count, 1
    )
    green_src = broadcast(green_piece, "rcv", src_index // src_per_rcv)
    row_tiles_count = rows_blk // TILE
    col_tiles_count = col_count // TILE
    tile_block = lax.dynamic_slice(
        tile_mask,
        (rcv_index * row_tiles_count, src_index * col_tiles_count),
        (row_tiles_count, col_tiles_count),
    )
    row_ids = rcv_index * row_tiles_count + jnp.arange(row_tiles_count)
    col_ids = src_index * col_tiles_count + jnp.arange(col_tiles_count)
    kept_tiles = tile_block == 1
    off_diag = kept_tiles & (row_ids[:, None] != col_ids[None, :])
    shaped = reflection.reshape(2, row_tiles_count, TILE, col_tiles_count, TILE)
    zero_value = jnp.zeros((), jnp.bfloat16)
    acquired = jnp.where(kept_tiles[None, :, None, :, None], shaped, zero_value).reshape(
        2, rows_blk, col_count
    )
    mirror_part = jnp.where(off_diag[None, :, None, :, None], shaped, zero_value).reshape(
        2, rows_blk, col_count
    )
    data_wide = jnp.concatenate([acquired[0], acquired[1], mirror_part[0], mirror_part[1]], axis=1)
    green_wide = jnp.concatenate([green_block[0], green_block[1]], axis=1)
    products = across(data_wide, green_wide)

    def quarter(row_slot, col_slot):
        return products[
            row_slot * col_count : (row_slot + 1) * col_count,
            col_slot * P_SIZE : (col_slot + 1) * P_SIZE,
        ]

    front_real = (quarter(0, 0) + quarter(1, 1)).astype(jnp.bfloat16)
    front_imag = (quarter(1, 0) - quarter(0, 1)).astype(jnp.bfloat16)
    back_real = (quarter(2, 0) - quarter(3, 1)).astype(jnp.bfloat16)
    back_imag = (quarter(3, 0) + quarter(2, 1)).astype(jnp.bfloat16)
    src_real = green_src[0]
    src_imag = green_src[1]
    green_stack = jnp.concatenate([src_real, src_imag], axis=0)
    mirror_left = jnp.concatenate(
        [
            jnp.concatenate([back_real, back_imag], axis=1),
            jnp.concatenate([back_imag, -back_real], axis=1),
        ],
        axis=0,
    )
    mirrored = across(green_stack, mirror_left)
    weights = jnp.concatenate(
        [
            jnp.concatenate([src_real, src_imag], axis=1),
            jnp.concatenate([-src_imag, src_real], axis=1),
        ],
        axis=0,
    )
    left_rows = jnp.concatenate([front_real, front_imag], axis=0)
    combined = across(left_rows, weights) + mirrored
    focal = lax.psum_scatter(combined, ("rcv", "src"), scatter_dimension=0, tiled=True)
    focal_real = focal[:, :P_SIZE]
    focal_imag = focal[:, P_SIZE:]
    chosen = jnp.arange(P_SIZE)[None, :] == reference_index[:, None]
    anchor_real = jnp.sum(jnp.where(chosen, focal_real, 0.0), axis=1)[:, None]
    anchor_imag = jnp.sum(jnp.where(chosen, focal_imag, 0.0), axis=1)[:, None]
    out_real = focal_real * anchor_real + focal_imag * anchor_imag
    out_imag = focal_imag * anchor_real - focal_real * anchor_imag
    return jnp.stack([out_real, out_imag], axis=1)


def solution(mesh):
    return jax.shard_map(
        body,
        mesh=mesh,
        in_specs=(P(None, "rcv", "src"), P(None, "rcv", "src"), P(), P(("rcv", "src"))),
        out_specs=P(("rcv", "src"), None, None),
        check_vma=False,
    )
```

profile of v0, /device:TPU:0, one launch (start us, length us, event | category | flops | bytes accessed | tf_op | source)
XLA Modules:
  0.0 491.1 jit_solution(2847651224598530955)
XLA Ops:
  6.5 0.0 all-gather.2.cloned.1.call-start
  6.5 0.7 all-gather.2.cloned.1.call-update
  7.3 0.0 all-reduce.2.cloned.1.call-start
  7.3 23.6 %copy.6 = bf16[1024,8,8,256]{3,2,1,0:T(8,128)(2,1)} copy(bf16[1024,8,8,256]{3,1,2,0:T(8,128)(2,1)} %bitcast.37) | data formatting | bytes 67108864
  30.9 0.8 compare_and_fusion
  31.7 32.3 %broadcast_select_fusion.1 = (bf16[2,16,256,8,256]{4,3,2,1,0:T(8,128)(2,1)}, bf16[2,16,256,8,256]{4,3,2,1,0:T(8,128)(2,1)}) fusion(bf16[2,16,256,8,256]{4,3,2,1,0:T(8,128)(2,1)} %bitcast.30, pred[16,8]{1,0:T(8,128)(4,1)S(1)} %get-tuple-element.10, pred[16,8]{1,0:T(8,128)(4,1)S(1)} %get-tuple-element.9), kind=kLoop, calls=%fused_computation.9 | loop fusion | flops 33554432 | bytes 100663552 | tf_op jit(solution)/shard_map/jit(_where)/select_n | solution.py:49
  64.0 38.8 %fusion.48 = (bf16[1,16,256,8,256]{4,3,2,1,0:T(8,128)(2,1)}, bf16[1,16,256,8,256]{4,3,2,1,0:T(8,128)(2,1)}, bf16[1,16,256,8,256]{4,3,2,1,0:T(8,128)(2,1)S(1)}, bf16[1,16,256,8,256]{4,3,2,1,0:T(8,128)(2,1)}) fusion(bf16[2,16,256,8,256]{4,3,2,1,0:T(8,128)(2,1)} %get-tuple-element.16, bf16[2,16,256,8,256]{4,3,2,1,0:T(8,128)(2,1)} %get-tuple-element.17), kind=kLoop, calls=%fused_computation.64 | loop fusion | bytes 134217728 | tf_op jit(solution)/shard_map/slice | solution.py:55
  102.8 16.3 %copy.7 = bf16[512,8,8,256]{3,1,2,0:T(8,128)(2,1)} copy(bf16[512,8,8,256]{3,2,1,0:T(8,128)(2,1)} %bitcast.36) | data formatting | bytes 33554432
  119.0 18.0 %copy.8 = bf16[512,8,8,256]{3,1,2,0:T(8,128)(2,1)} copy(bf16[512,8,8,256]{3,2,1,0:T(8,128)(2,1)} %bitcast.35) | data formatting | bytes 33554432
  137.1 0.0 slice-done
  137.1 0.0 slice-done.2
  137.1 9.8 %copy.9 = bf16[512,8,8,256]{3,1,2,0:T(8,128)(2,1)} copy(bf16[512,8,8,256]{3,2,1,0:T(8,128)(2,1)S(1)} %bitcast.34) | data formatting | bytes 33554432
  146.8 9.7 %copy.10 = bf16[512,8,8,256]{3,1,2,0:T(8,128)(2,1)} copy(bf16[512,8,8,256]{3,2,1,0:T(8,128)(2,1)S(1)} %bitcast.31) | data formatting | bytes 33554432
  156.6 5.6 %dynamic-slice_select_fusion = bf16[2,2048,512]{1,2,0:T(8,128)(2,1)} fusion(bf16[2,4096,512]{1,2,0:T(8,128)(2,1)} %all-gather.2.cloned.1.call-done, s32[]{:T(128)S(6)} %select_n.49, pred[]{:T(512)S(6)} %eq.26), kind=kLoop, calls=%fused_computation.45 | loop fusion | flops 2097152 | bytes 8388613 | tf_op jit(solution)/shard_map/jit(_where)/select_n | solution.py:11
  162.1 0.0 all-reduce.2.cloned.1.call-update
  162.1 0.2 reduce-scatter.2.cloned.1.call-start
  162.4 6.0 %slice_bitcast_fusion.1 = (bf16[4096,512]{0,1:T(8,128)(2,1)}, bf16[4096,512]{0,1:T(8,128)(2,1)}) fusion(bf16[2,4096,512]{1,2,0:T(8,128)(2,1)} %all-gather.2.cloned.1.call-done), kind=kLoop, calls=%fused_computation.38 | loop fusion | bytes 16777216 | tf_op jit(solution)/shard_map/squeeze | solution.py:56
  168.3 107.8 %fusion = f32[8192,1024]{0,1:T(8,128)} fusion(bf16[4096,2048]{1,0:T(8,128)(2,1)} %bitcast.41, bf16[4096,2048]{1,0:T(8,128)(2,1)} %bitcast.40, bf16[4096,2048]{1,0:T(8,128)(2,1)} %bitcast.39, bf16[4096,2048]{1,0:T(8,128)(2,1)} %bitcast.38, bf16[4096,512]{0,1:T(8,128)(2,1)} %get-tuple-element.21, bf16[4096,512]{0,1:T(8,128)(2,1)} %get-tuple-element.20), kind=kOutput, calls=%fused_computation | convolution fusion | flops 69004689408 | bytes 109051904 | tf_op jit(solution)/shard_map/dot_general | solution.py:16
  276.1 6.0 %fusion.46 = (bf16[2048,512]{0,1:T(8,128)(2,1)S(1)}, bf16[2048,512]{0,1:T(8,128)(2,1)}) fusion(f32[8192,1024]{0,1:T(8,128)} %fusion), kind=kLoop, calls=%fused_computation.63 | loop fusion | flops 3145728 | bytes 12582912 | tf_op jit(solution)/shard_map/neg | solution.py:75
  282.1 11.8 %fusion.27 = (bf16[2048,512]{0,1:T(8,128)(2,1)}, bf16[2048,512]{0,1:T(8,128)(2,1)}, bf16[2048,512]{0,1:T(8,128)(2,1)}) fusion(f32[8192,1024]{0,1:T(8,128)} %fusion), kind=kLoop, calls=%fused_computation.30 | loop fusion | flops 6291456 | bytes 31457280 | tf_op jit(solution)/shard_map/convert_element_type | solution.py:68
  293.9 25.8 %all-reduce.2.cloned.1.call-done = bf16[2,2048,512]{1,2,0:T(8,128)(2,1)} async-done(((bf16[2,2048,512]{1,2,0:T(8,128)(2,1)}), bf16[2,2048,512]{1,2,0:T(8,128)(2,1)}) %all-reduce.2.cloned.1.call-update) | async-done | bytes 4194320 | tf_op jit(solution)/shard_map/psum | solution.py:12
  319.8 4.9 %slice_bitcast_fusion.2 = (bf16[2048,512]{0,1:T(8,128)(2,1)}, bf16[2048,512]{0,1:T(8,128)(2,1)}) fusion(bf16[2,2048,512]{1,2,0:T(8,128)(2,1)} %all-reduce.2.cloned.1.call-done), kind=kLoop, calls=%fused_computation.46 | loop fusion | bytes 8388608 | tf_op jit(solution)/shard_map/squeeze | solution.py:70
  324.7 0.0 copy-done
  324.7 0.1 fusion.45
  324.8 0.0 copy-start.1
  324.8 10.1 %fusion.11 = f32[512,1024]{1,0:T(8,128)} fusion(bf16[2048,512]{0,1:T(8,128)(2,1)} %get-tuple-element.23, bf16[2048,512]{0,1:T(8,128)(2,1)S(1)} %fusion.45, bf16[2048,512]{0,1:T(8,128)(2,1)} %get-tuple-element.22, bf16[2048,512]{0,1:T(8,128)(2,1)} %get-tuple-element.12, bf16[2048,512]{0,1:T(8,128)(2,1)} %get-tuple-element.13), kind=kOutput, calls=%fused_computation.13 | convolution fusion | flops 4336910336 | bytes 12582912 | tf_op jit(solution)/shard_map/dot_general | solution.py:16
  334.9 9.9 %fusion.37 = f32[512,1024]{1,0:T(8,128)} fusion(f32[512,1024]{1,0:T(8,128)} %fusion.11, bf16[2048,512]{0,1:T(8,128)(2,1)S(1)} %get-tuple-element.7, bf16[2048,512]{0,1:T(8,128)(2,1)} %get-tuple-element.11, bf16[2048,512]{0,1:T(8,128)(2,1)S(1)} %copy-done.1, bf16[2048,512]{0,1:T(8,128)(2,1)} %get-tuple-element.22, bf16[2048,512]{0,1:T(8,128)(2,1)} %get-tuple-element.23), kind=kOutput, calls=%fused_computation.48 | convolution fusion | flops 4337434624 | bytes 14680064 | tf_op jit(solution)/shard_map/dot_general | solution.py:16
  344.9 0.0 reduce-scatter.2.cloned.1.call-update
  344.9 137.1 %reduce-scatter.2.cloned.1.call-done = f32[16,1024]{1,0:T(8,128)} async-done(((f32[512,1024]{1,0:T(8,128)}), f32[16,1024]{1,0:T(8,128)}) %reduce-scatter.2.cloned.1.call-update) | async-done | bytes 65552 | tf_op jit(solution)/shard_map/reduce_scatter | solution.py:89
  482.0 1.0 select_reduce_fusion.1
  483.0 0.9 add_bitcast_fusion
  483.8 0.7 copy.5
  (15 shorter events, 0.0 us)
Async XLA Ops:
  6.5 150.0 %all-gather.2.cloned.1.call-start = ((), (), s32[]{:S(2)}) async-start(), calls=%async_computation.1 | async-start | bytes 9437184 | tf_op jit(solution)/shard_map/all_gather | solution.py:30
  7.3 312.5 %all-reduce.2.cloned.1.call-start = ((), (), s32[]{:S(2)}) async-start(), calls=%async_computation.2 | async-start | bytes 8388608 | tf_op jit(solution)/shard_map/psum | solution.py:12
  119.0 18.0 %slice-start = ((s8[16777216]{0:T(1024)(128)(4,1)}), s8[4194304]{0:T(1024)(128)(4,1)S(1)}, s32[]{:S(2)}) async-start(s8[16777216]{0:T(1024)(128)(4,1)} %bitcast.32), calls=%async_computation.4 | async-start | bytes 8388608
  119.0 18.0 %slice-start.1 = ((s8[16777216]{0:T(1024)(128)(4,1)}), s8[4194304]{0:T(1024)(128)(4,1)S(1)}, s32[]{:S(2)}) async-start(s8[16777216]{0:T(1024)(128)(4,1)} %bitcast.32), calls=%async_computation.5 | async-start | bytes 8388608
  119.0 18.0 %slice-start.2 = ((s8[16777216]{0:T(1024)(128)(4,1)}), s8[4194304]{0:T(1024)(128)(4,1)S(1)}, s32[]{:S(2)}) async-start(s8[16777216]{0:T(1024)(128)(4,1)} %bitcast.32), calls=%async_computation.6 | async-start | bytes 8388608
  119.0 18.0 %slice-start.3 = ((s8[16777216]{0:T(1024)(128)(4,1)}), s8[4194304]{0:T(1024)(128)(4,1)S(1)}, s32[]{:S(2)}) async-start(s8[16777216]{0:T(1024)(128)(4,1)} %bitcast.32), calls=%async_computation.7 | async-start | bytes 8388608
  162.1 319.9 %reduce-scatter.2.cloned.1.call-start = ((), (), s32[]{:S(2)}) async-start(), calls=%async_computation.3 | async-start | bytes 2162688 | tf_op jit(solution)/shard_map/reduce_scatter | solution.py:89
  319.8 4.9 %copy-start = (bf16[2,2048,512]{1,2,0:T(8,128)(2,1)S(1)}, bf16[2,2048,512]{1,2,0:T(8,128)(2,1)}, u32[]{:S(2)}) copy-start(bf16[2,2048,512]{1,2,0:T(8,128)(2,1)} %all-reduce.2.cloned.1.call-done) | copy-start | bytes 12582916
  324.8 10.1 %copy-start.1 = (bf16[2048,512]{0,1:T(8,128)(2,1)S(1)}, bf16[2048,512]{0,1:T(8,128)(2,1)}, u32[]{:S(2)}) copy-start(bf16[2048,512]{0,1:T(8,128)(2,1)} %get-tuple-element.8) | copy-start | bytes 6291460
  334.9 147.1 %copy-start.2 = (s32[16]{0:T(128)S(1)}, s32[16]{0:T(128)}, u32[]{:S(2)}) copy-start(s32[16]{0:T(128)} %param.7) | copy-start | bytes 196
Sparse Core Ops, SparseCore 0:
  9.2 56.9 all-gather.1
  162.3 157.4 all-reduce.1
  345.0 136.9 reduce-scatter.1
where the time goes:
time: 491 us
  waiting for transfers between devices  164 us (33%)
  local copies, waits for them, and re-layouts  128 us (26%)
  matrix products  128 us (26%)
  other arithmetic  58.4 us (12%)
  between operations  13.2 us (3%)
    reduce_scatter x1, waiting for transfers between devices, body(): lax.psum_scatter(combined, ('rcv', 'src'), scatter_dimension=0, tiled=True)  137 us
    dot_general x3, matrix products, across(): lax.dot_general(first, second, (((0,), (0,)), ((), ())), precision=precis...  128 us
    unnamed x19, local copies, waits for them, and re-layouts  77.4 us
    slice x1, local copies, waits for them, and re-layouts, body(): acquired[0]  38.8 us
    select_n x1, other arithmetic, body(): jnp.where(kept_tiles[None, :, None, :, None], shaped, zero_value)  32.3 us
    psum x1, waiting for transfers between devices, broadcast(): return lax.psum(block, axis)  25.8 us
    convert_element_type x1, other arithmetic, body(): back_imag = (quarter(3, 0) + quarter(2, 1)).astype(jnp.bfloat16)  11.8 us
  transfers between devices with their start and end apart: 3, of which 2 were waited for; matrix products, arithmetic and copies ran while one was open for 57% of the time, Pallas kernels for 0%

commit v1 on v0

v1 whole, which is shorter than its diff:
```python
import functools

import jax
import jax.numpy as jnp
from jax import lax
from jax.experimental import pallas as pl
from jax.experimental.pallas import tpu as pltpu
from jax.sharding import PartitionSpec as P

MESH = pl.DeviceIdType.MESH
TILE = 256
f32 = jnp.float32
bf16 = jnp.bfloat16


def dot_nn(a, b):
    return lax.dot_general(a, b, (((1,), (0,)), ((), ())), preferred_element_type=f32)


def dot_nt(a, b):
    return lax.dot_general(a, b, (((1,), (1,)), ((), ())), preferred_element_type=f32)


def kernel(
    n_rcv, n_src, mask_ref, piece_ref, refl_ref, focal_ref,
    gr, gc, y, abuf, acc, quad, slab, arrived,
    gr_send, fw_send, gr_recv, gc_send, gc_recv, gc_local, own_sem, load_sem, slab_send, slab_recv,
):
    n_dev = n_rcv * n_src
    r = lax.axis_index("rcv")
    s = lax.axis_index("src")
    me = r * n_src + s
    partner = s + 1 - 2 * lax.rem(s, 2)
    n_p, rows = gr.shape[1], gr.shape[2]
    cols = gc.shape[2]
    own_p = n_p // n_src
    out_rows = n_p // n_dev
    n_tiles = cols // TILE
    row_tiles = rows // TILE

    def last_col(src):
        return (src + 1) * cols

    def is_active(rcv, src):
        return rcv * rows < last_col(src)

    def pair_active(rcv, src):
        return rcv * rows < last_col(src - lax.rem(src, 2) + 1)

    active = is_active(r, s)
    gathers = pair_active(r, s)
    holder = (s * cols) // rows
    offset = pl.multiple_of(s * cols - holder * rows, TILE)
    on_diag = r == holder

    def load(t):
        slot = lax.rem(t, 2)
        return pltpu.make_async_copy(
            refl_ref.at[:, :, pl.ds(pl.multiple_of(t * TILE, TILE), TILE)],
            abuf.at[slot],
            load_sem.at[slot],
        )

    def gr_slot(i):
        return gr.at[:, pl.ds(pl.multiple_of(i * own_p, own_p), own_p), :]

    def gc_slot(i):
        return gc.at[:, pl.ds(pl.multiple_of(i * own_p, own_p), own_p), :]

    own_copy = pltpu.make_async_copy(piece_ref, gr_slot(s), own_sem)

    @pl.when(active)
    def _():
        load(0).start()

    @pl.when(gathers)
    def _():
        own_copy.start()

    barrier = pltpu.get_barrier_semaphore()

    @pl.loop(1, n_dev)
    def _(i):
        other = lax.rem(me + i, n_dev)
        pl.semaphore_signal(
            barrier, inc=1, device_id=(other // n_src, lax.rem(other, n_src)), device_id_type=MESH
        )

    pl.semaphore_wait(barrier, n_dev - 1)

    def piece_to(dest):
        return pltpu.make_async_remote_copy(
            src_ref=piece_ref, dst_ref=gr_slot(s), send_sem=gr_send.at[dest], recv_sem=gr_recv.at[s],
            device_id=(r, dest), device_id_type=MESH,
        )

    def forward(i):
        return pltpu.make_async_remote_copy(
            src_ref=gr_slot(i), dst_ref=gr_slot(i), send_sem=fw_send.at[i], recv_sem=gr_recv.at[i],
            device_id=(r, partner), device_id_type=MESH,
        )

    def upward(i):
        return lax.rem(i // 2, 2) == 1

    def source_target(i):
        return jnp.where(upward(i), 0, r - 1)

    def from_source(i):
        return pltpu.make_async_remote_copy(
            src_ref=gr.at[:, pl.ds(pl.multiple_of(i * own_p, own_p), own_p), pl.ds(offset, cols)],
            dst_ref=gc_slot(i), send_sem=gc_send.at[i], recv_sem=gc_recv.at[i],
            device_id=(source_target(i), s), device_id_type=MESH,
        )

    def to_local(i):
        return pltpu.make_async_copy(
            gr.at[:, pl.ds(pl.multiple_of(i * own_p, own_p), own_p), pl.ds(offset, cols)],
            gc_slot(i), gc_local.at[i],
        )

    def relay(i):
        return pltpu.make_async_remote_copy(
            src_ref=gc_slot(i), dst_ref=gc_slot(i), send_sem=gc_send.at[i], recv_sem=gc_recv.at[i],
            device_id=(jnp.where(upward(i), r + 1, r - 1), s), device_id_type=MESH,
        )

    def relays(i):
        return (jnp.logical_not(upward(i)) & (r >= 1)) | (upward(i) & (r + 1 < holder))

    def share(i):
        @pl.when(on_diag)
        def _():
            to_local(i).start()

            @pl.when(r >= 1)
            def _():
                from_source(i).start()

    same = [lax.rem(s + 2 * i, n_src) for i in range(1, n_src // 2)]
    for dest in same:
        @pl.when(pair_active(r, dest))
        def _():
            piece_to(dest).start()

    @pl.when(gathers)
    def _():
        piece_to(partner).start()
        own_copy.wait()
        share(s)
        forward(partner).wait_recv()
        share(partner)
        for i in same:
            forward(i).wait_recv()
            forward(i).start()
            share(i)
        for i in same:
            twin = i + 1 - 2 * lax.rem(i, 2)
            forward(twin).wait_recv()
            share(twin)

    per = -(-n_src // n_tiles)
    step_rows = min(rows, 1024)

    @pl.when(active)
    def _():
        @pl.loop(0, n_tiles)
        def _(t):
            slot = lax.rem(t, 2)
            load(t).wait()

            @pl.when(t + 1 < n_tiles)
            def _():
                load(t + 1).start()

            for i in range(per):
                p = t * per + i

                @pl.when((p < n_src) & jnp.logical_not(on_diag))
                def _():
                    relay(p).wait_recv()

                    @pl.when(relays(p))
                    def _():
                        relay(p).start()

            col_end = s * cols + (t + 1) * TILE
            for k in range(rows // step_rows):
                def step():
                    for j in range(step_rows // TILE):
                        m = mask_ref[k * (step_rows // TILE) + j, t]
                        at = pl.ds(k * step_rows + j * TILE, TILE)
                        for z in range(2):
                            tile = abuf[slot, z, at, :]
                            abuf[slot, z, at, :] = jnp.where(m == 1, tile, jnp.zeros_like(tile))
                    left = gr[:, :, k * step_rows:(k + 1) * step_rows].reshape(2 * n_p, step_rows)
                    for z in range(2):
                        term = dot_nn(left, abuf[slot, z, k * step_rows:(k + 1) * step_rows, :])
                        if k == 0:
                            acc[z] = term
                        else:
                            acc[z] += term

                if k == 0:
                    step()
                else:
                    pl.when(r * rows + k * step_rows < col_end)(step)
            at = pl.ds(pl.multiple_of(t * TILE, TILE), TILE)
            for z in range(2):
                y[z, :, at] = acc[z].astype(bf16)

        @pl.when(on_diag)
        def _():
            @pl.loop(0, n_src)
            def _(i):
                to_local(i).wait()

        def second(direct):
            @pl.loop(0, n_p // TILE)
            def _(b):
                at = pl.ds(pl.multiple_of(b * TILE, TILE), TILE)
                g_re = gc[0, at, :]
                g_im = gc[1, at, :]
                s_re = dot_nt(y[0, :n_p, :], g_re) + dot_nt(y[0, n_p:, :], g_im)
                k_im = dot_nt(y[1, :n_p, :], g_im) - dot_nt(y[1, n_p:, :], g_re)
                if direct:
                    quad[0, :, at] = s_re - k_im
                quad[2, :, at] = s_re + k_im
                s_im = dot_nt(y[1, :n_p, :], g_re) + dot_nt(y[1, n_p:, :], g_im)
                k_re = dot_nt(y[0, :n_p, :], g_im) - dot_nt(y[0, n_p:, :], g_re)
                if direct:
                    quad[1, :, at] = s_im + k_re
                quad[3, :, at] = s_im - k_re

        second(True)

        first_tile = s * n_tiles - r * row_tiles
        overlaps = (first_tile < row_tiles) & (first_tile + n_tiles > 0)

        @pl.when(overlaps)
        def _():
            @pl.loop(0, n_tiles)
            def _(t):
                row = first_tile + t

                @pl.when((row >= 0) & (row < row_tiles))
                def _():
                    at_r = pl.ds(pl.multiple_of(row * TILE, TILE), TILE)
                    at_c = pl.ds(pl.multiple_of(t * TILE, TILE), TILE)
                    tile_copy = pltpu.make_async_copy(
                        refl_ref.at[:, at_r, at_c], abuf.at[0, :, pl.ds(0, TILE), :], own_sem
                    )
                    tile_copy.start()
                    tile_copy.wait()
                    m = mask_ref[row, t]
                    left = gr[:, :, at_r].reshape(2 * n_p, TILE)
                    for z in range(2):
                        tile = abuf[0, z, :TILE, :]
                        tile = jnp.where(m == 1, tile, jnp.zeros_like(tile))
                        kept = y[z, :, at_c].astype(f32) - dot_nn(left, tile)
                        y[z, :, at_c] = kept.astype(bf16)

            second(False)

        for part in range(2):
            for b in range(n_p // TILE):
                turned = quad[2 + part, :, b * TILE:(b + 1) * TILE].T
                quad[part, b * TILE:(b + 1) * TILE, :] += turned

        group = max(16, out_rows)

        @pl.loop(0, n_p // group)
        def _(g):
            at = pl.ds(pl.multiple_of(g * group, group), group)
            for part in range(2):
                block = quad[part, at, :]
                for j in range(group // out_rows):
                    slab[g * (group // out_rows) + j, :, part * n_p:(part + 1) * n_p] = block[
                        j * out_rows:(j + 1) * out_rows
                    ].astype(bf16)

    def slab_to(other):
        return pltpu.make_async_remote_copy(
            src_ref=slab.at[other], dst_ref=arrived.at[me], send_sem=slab_send.at[other],
            recv_sem=slab_recv.at[me],
            device_id=(other // n_src, lax.rem(other, n_src)), device_id_type=MESH,
        )

    def slab_from(other):
        return pltpu.make_async_remote_copy(
            src_ref=slab.at[me], dst_ref=arrived.at[other], send_sem=slab_send.at[other],
            recv_sem=slab_recv.at[other],
            device_id=(other // n_src, lax.rem(other, n_src)), device_id_type=MESH,
        )

    @pl.when(active)
    def _():
        @pl.loop(1, n_dev)
        def _(i):
            slab_to(lax.rem(me + i, n_dev)).start()

    focal_ref[...] = jnp.zeros_like(focal_ref)

    @pl.when(active)
    def _():
        focal_ref[...] = slab[me].astype(f32)

    for other in range(n_dev):
        if (other // n_src) * rows < (other % n_src + 1) * cols:
            @pl.when(me != other)
            def _():
                slab_from(other).wait_recv()
                focal_ref[...] += arrived[other].astype(f32)

    @pl.when(active)
    def _():
        @pl.loop(1, n_dev)
        def _(i):
            slab_to(lax.rem(me + i, n_dev)).wait_send()

    for dest in same:
        @pl.when(pair_active(r, dest))
        def _():
            piece_to(dest).wait_send()

    @pl.when(gathers)
    def _():
        piece_to(partner).wait_send()
        for i in same:
            forward(i).wait_send()

        @pl.loop(0, n_src)
        def _(i):
            @pl.when(on_diag & (r >= 1))
            def _():
                from_source(i).wait_send()

            @pl.when(active & jnp.logical_not(on_diag) & relays(i))
            def _():
                relay(i).wait_send()


def body(reflection, green, tile_mask, reference_index):
    rows, cols = reflection.shape[1], reflection.shape[2]
    n_rcv, n_src = lax.axis_size("rcv"), lax.axis_size("src")
    n_dev = n_rcv * n_src
    own_p = green.shape[2]
    n_p = own_p * n_src
    out_rows = n_p // n_dev
    r, s = lax.axis_index("rcv"), lax.axis_index("src")
    row_tiles, n_tiles = rows // TILE, cols // TILE
    tile_block = lax.dynamic_slice(tile_mask, (r * row_tiles, s * n_tiles), (row_tiles, n_tiles))
    piece = jnp.swapaxes(green, 1, 2)
    dma = pltpu.SemaphoreType.DMA
    any_spec = pl.BlockSpec(memory_space=pl.ANY)
    focal = pl.pallas_call(
        functools.partial(kernel, n_rcv, n_src),
        out_shape=jax.ShapeDtypeStruct((out_rows, 2 * n_p), f32),
        in_specs=[pl.BlockSpec(memory_space=pltpu.SMEM), any_spec, any_spec],
        out_specs=pl.BlockSpec(memory_space=pltpu.VMEM),
        scratch_shapes=[
            pltpu.VMEM((2, n_p, rows), bf16),
            pltpu.VMEM((2, n_p, cols), bf16),
            pltpu.VMEM((2, 2 * n_p, cols), bf16),
            pltpu.VMEM((2, 2, rows, TILE), bf16),
            pltpu.VMEM((2, 2 * n_p, TILE), f32),
            pltpu.VMEM((4, n_p, n_p), f32),
            pltpu.VMEM((n_dev, out_rows, 2 * n_p), bf16),
            pltpu.VMEM((n_dev, out_rows, 2 * n_p), bf16),
            dma((n_src,)), dma((n_src,)), dma((n_src,)), dma((n_src,)), dma((n_src,)), dma((n_src,)),
            dma, dma((2,)), dma((n_dev,)), dma((n_dev,)),
        ],
        compiler_params=pltpu.CompilerParams(
            collective_id=0, has_side_effects=True, vmem_limit_bytes=60 * 1024 * 1024
        ),
        name="focus",
    )(tile_block, piece, reflection)
    focal_real = focal[:, :n_p]
    focal_imag = focal[:, n_p:]
    chosen = jnp.arange(n_p)[None, :] == reference_index[:, None]
    anchor_real = jnp.sum(jnp.where(chosen, focal_real, 0.0), axis=1)[:, None]
    anchor_imag = jnp.sum(jnp.where(chosen, focal_imag, 0.0), axis=1)[:, None]
    out_real = focal_real * anchor_real + focal_imag * anchor_imag
    out_imag = focal_imag * anchor_real - focal_real * anchor_imag
    return jnp.stack([out_real, out_imag], axis=1)


def solution(mesh):
    return jax.shard_map(
        body,
        mesh=mesh,
        in_specs=(P(None, "rcv", "src"), P(None, "rcv", "src"), P(), P(("rcv", "src"))),
        out_specs=P(("rcv", "src"), None, None),
        check_vma=False,
    )
```

time: 491 us -> 284 us (0.58)
  Pallas kernels: 0 us -> 278 us
  waiting for transfers between devices: 164 us -> 0 us
  matrix products: 128 us -> 0 us
  local copies, waits for them, and re-layouts: 128 us -> 2.07 us
  other arithmetic: 58.4 us -> 1.82 us
  between operations: 13.2 us -> 0.03 us
    pallas_call x0 -> x1, Pallas kernels: none -> 278 us  [body(): pl.pallas_call(functools.partial(kernel, n_rcv, n_src), out_shape=jax.Sha...]
    reduce_scatter x1 -> x0, waiting for transfers between devices: 137 us -> none  [body(): lax.psum_scatter(combined, ('rcv', 'src'), scatter_dimension=0, tiled=True)]
    dot_general x3 -> x0, matrix products: 128 us -> none  [across(): lax.dot_general(first, second, (((0,), (0,)), ((), ())), precision=precis...]
    unnamed x19 -> x2, local copies, waits for them, and re-layouts: 77.4 us -> 0.01 us
    slice x1 -> x0, local copies, waits for them, and re-layouts: 38.8 us -> none  [body(): acquired[0]]
    select_n x2 -> x0, other arithmetic: 37.9 us -> none  [the longest x1 32.3 us: body(): jnp.where(kept_tiles[None, :, None, :, None], shaped, zero_value)]
    psum x1 -> x0, waiting for transfers between devices: 25.8 us -> none  [broadcast(): return lax.psum(block, axis)]
    convert_element_type x1 -> x0, other arithmetic: 11.8 us -> none  [body(): back_imag = (quarter(3, 0) + quarter(2, 1)).astype(jnp.bfloat16)]
  transfers between devices with their start and end apart: 3 -> 0, of which waited for: 2 -> 0; matrix products, arithmetic and copies ran while one was open for 57% -> 0% of each run, Pallas kernels for 0% -> 0%
where the time goes in v1:
time: 284 us; the launch traced here: 282 us
  Pallas kernels  278 us (98%)
    pallas_call x1, Pallas kernels, body(): pl.pallas_call(functools.partial(kernel, n_rcv, n_src), out_shape=jax.Sha...  278 us

profile of v1, /device:TPU:0, one launch (start us, length us, event | category | flops | bytes accessed | tf_op | source)
XLA Modules:
  0.0 281.8 jit_solution(10046186792850499356)
XLA Ops:
  0.0 0.0 copy-start
  0.0 1.4 dynamic_slice.3.mask_ref
  1.4 277.8 %focus.1 = f32[16,1024]{1,0:T(8,128)} custom-call(s32[16,8]{1,0:T(8,128)} %dynamic_slice.3.mask_ref, bf16[2,64,4096]{2,1,0:T(8,128)(2,1)} %bitcast.5, bf16[2,4096,2048]{2,1,0:T(8,128)(2,1)} %refl_ref.1), custom_call_target="tpu_custom_call" | custom-call | tf_op jit(solution)/shard_map/focus/pallas_call | solution.py:356
  279.2 0.0 copy-done
  279.2 1.0 select_reduce_fusion.1
  280.2 0.9 add_bitcast_fusion
  281.1 0.7 copy.5
  (1 shorter events, 0.0 us)
Async XLA Ops:
  0.0 279.2 %copy-start = (s32[16]{0:T(128)S(1)}, s32[16]{0:T(128)}, u32[]{:S(2)}) copy-start(s32[16]{0:T(128)} %param.7) | copy-start | bytes 196
